TPU v7x, 32 devices: a whole 2x2x4 slice. The times are simulated.
32 devices in a mesh: dp: 2 (over core), blk: 4 (over y, x), rep: 4 (over z).
Axes of the slice: x: 2, y: 2, z: 4, core: 2. Of those that a mesh axis runs over, the one named last changes fastest.
Arguments:
- feats: bfloat16 [2, 16384, 512], P('dp', ('blk', 'rep')), may hold values from -6 to 6
- weight: bfloat16 [512, 512], replicated, may hold values from -0.25 to 0.25
- cols: int32 [2, 128, 15], P('dp', ('blk', 'rep')), may hold values from -1 to 127, as said below
- vals: bfloat16 [2, 128, 15, 128, 128], P('dp', ('blk', 'rep')), as said below
- cotangent: bfloat16 [2, 16384, 512], P('dp', ('blk', 'rep')), may hold values from -6 to 6
Outputs:
- activ: bfloat16 [2, 16384, 512], P('dp', ('blk', 'rep'))
- feat_grad: bfloat16 [2, 16384, 512], P('dp', ('blk', 'rep'))
- weight_grad: float32 [512, 512], replicated
Inputs may be any that keep to these rules, and one draw needn't show every extreme that they name: `cols`: used slots come first in each row and -1 marks the unused ones. Slot 0 of block row p names p itself; every other used slot names a block at most 7 away from p, each at most once. The relation is symmetric: p names q exactly when q names p. In every scenario some block row uses all 15 slots. `vals`: the block in row p's slot naming q is the transpose of the block in row q's slot naming p (the self block is symmetric); unused slots hold zeros.
All inputs are finite; a program needn't handle non-finite values.
Results may differ from a plain program's by a relative error of at most 0.0061.
Values may be sent and summed in bfloat16 or wider, within the bound.
No kernel may reach another device: no remote copies, remote signals or barrier semaphores. Data moves between devices by JAX's collectives and lax.ppermute only.
A program may use at most 128 MiB of HBM per device.

v0:
```python
import jax
import jax.numpy as jnp
from jax import lax
from jax.sharding import PartitionSpec as P

REACH = 7


def padded(cells, sides, width):
    for axis, dim in sides:
        count = lax.axis_size(axis)
        ends = count - 1
        head = lax.slice_in_dim(cells, 0, width, axis=dim)
        tail = lax.slice_in_dim(cells, cells.shape[dim] - width, cells.shape[dim], axis=dim)
        cells = jnp.concatenate(
            [
                lax.ppermute(tail, axis, [(i, (i + 1) % count) for i in range(ends)]),
                cells,
                lax.ppermute(head, axis, [((i + 1) % count, i) for i in range(ends)]),
            ],
            axis=dim,
        )
    return cells


def spread(extended, row_cols, row_vals, first):
    row_blocks = row_vals.shape[0]
    block_size = row_vals.shape[2]
    width = extended.shape[1]
    ext_blocks = extended.reshape(-1, block_size, width)
    margin = (ext_blocks.shape[0] - row_blocks) // 2
    local_index = jnp.where(row_cols >= 0, row_cols - first + margin, 0)
    picked = ext_blocks[local_index]
    summed = jnp.einsum("rkab,rkbf->raf", row_vals, picked, preferred_element_type=jnp.float32)
    return summed.reshape(-1, width)


def shards(feats, weight, cols, vals, cotangent):
    first = lax.axis_index(("blk", "rep")) * cols.shape[1]
    rim_rows = REACH * vals.shape[3]
    own = feats[0]
    projected = jnp.dot(own, weight, preferred_element_type=jnp.float32).astype(jnp.bfloat16)
    extended = padded(projected, ((("blk", "rep"), 0),), rim_rows)
    agg = spread(extended, cols[0], vals[0], first)
    sig = jax.nn.sigmoid(agg)
    activ_list = [(agg * sig).astype(jnp.bfloat16)]
    dagg = (cotangent[0].astype(jnp.float32) * sig * (1.0 + agg * (1.0 - sig))).astype(jnp.bfloat16)
    grad_ext = padded(dagg, ((("blk", "rep"), 0),), rim_rows)
    dproj = spread(grad_ext, cols[0], vals[0], first).astype(jnp.bfloat16)
    back = lax.dot_general(
        dproj, weight, (((1,), (1,)), ((), ())), preferred_element_type=jnp.float32
    )
    grad_list = [back.astype(jnp.bfloat16)]
    grads = lax.dot_general(
        own, dproj, (((0,), (0,)), ((), ())), preferred_element_type=jnp.float32
    )
    weight_grad = lax.psum(grads, ("dp", "blk", "rep"))
    return (jnp.stack(activ_list), jnp.stack(grad_list), weight_grad)


def solution(mesh):
    placed = (
        P("dp", ("blk", "rep"), None),
        P(),
        P("dp", ("blk", "rep"), None),
        P("dp", ("blk", "rep"), None, None, None),
        P("dp", ("blk", "rep"), None),
    )
    return jax.shard_map(
        shards,
        mesh=mesh,
        in_specs=placed,
        out_specs=(P("dp", ("blk", "rep"), None), P("dp", ("blk", "rep"), None), P()),
        check_vma=False,
    )
```

profile of v0, /device:TPU:0, one launch (start us, length us, event | category | flops | bytes accessed | tf_op | source)
XLA Modules:
  0.0 287.8 jit_solution(11901660477694064899)
XLA Ops:
  7.2 1.2 copy-done
  8.4 1.7 convolution_convert_fusion.1
  10.1 1.1 fusion.16
  11.2 5.9 %collective-permute-start = (bf16[896,512]{1,0:T(8,128)(2,1)}, bf16[896,512]{1,0:T(8,128)(2,1)}, u32[]{:S(2)}, u32[]{:S(2)}) collective-permute-start(bf16[896,512]{1,0:T(8,128)(2,1)} %get-tuple-element.8), channel_id=1, source_target_pairs={{0,1},{1,2},{2,3},{3,4},{4,5},{5,6},{6,7},{7,8},{8,9},{9,10},{10,1... | collective-permute-start | bytes 2752520 | tf_op jit(solution)/shard_map/ppermute | solution.py:17
  17.1 1.3 collective-permute-start.1
  18.5 17.5 %collective-permute-done = bf16[896,512]{1,0:T(8,128)(2,1)} collective-permute-done((bf16[896,512]{1,0:T(8,128)(2,1)}, bf16[896,512]{1,0:T(8,128)(2,1)}, u32[]{:S(2)}, u32[]{:S(2)}) %collective-permute-start) | collective-permute-done | bytes 917536 | tf_op jit(solution)/shard_map/ppermute | solution.py:17
  36.1 23.3 %collective-permute-done.1 = bf16[896,512]{1,0:T(8,128)(2,1)} collective-permute-done((bf16[896,512]{1,0:T(8,128)(2,1)S(1)}, bf16[896,512]{1,0:T(8,128)(2,1)}, u32[]{:S(2)}, u32[]{:S(2)}) %collective-permute-start.1) | collective-permute-done | bytes 917536 | tf_op jit(solution)/shard_map/ppermute | solution.py:19
  59.3 3.2 %pad_maximum_fusion = bf16[2816,512]{1,0:T(8,128)(2,1)} fusion(bf16[896,512]{1,0:T(8,128)(2,1)} %collective-permute-done.1, bf16[1024,512]{1,0:T(8,128)(2,1)S(1)} %convolution_convert_fusion.1, bf16[896,512]{1,0:T(8,128)(2,1)} %collective-permute-done), kind=kLoop, calls=%fused_computation.6 | loop fusion | flops 8650752 | bytes 5767168 | tf_op jit(solution)/shard_map/concatenate | solution.py:15
  62.6 9.5 %gather_fusion = bf16[120,128,512]{2,1,0:T(8,128)(2,1)} fusion(bf16[22,128,512]{2,1,0:T(8,128)(2,1)} %bitcast.62, s32[1024]{0:T(1024)S(1)} %pad_clamp_fusion), kind=kCustom, calls=%fused_computation | custom fusion | bytes 31457760 | tf_op jit(solution)/shard_map/gather | solution.py:33
  72.1 8.2 %fusion = f32[8,512,128,1]{1,2,3,0:T(8,128)S(1)} fusion(bf16[8,15,128,512]{3,2,1,0:T(8,128)(2,1)} %bitcast.64, bf16[1,8,15,128,128]{4,3,2,1,0:T(8,128)(2,1)} %param.8), kind=kOutput, calls=%fused_computation.2 | convolution fusion | flops 2013265920 | bytes 21757952 | tf_op jit(solution)/shard_map/rkab,rkbf->raf/dot_general | solution.py:34
  80.3 0.8 fusion.5
  81.3 2.5 collective-permute-start.2
  83.8 1.3 collective-permute-start.3
  85.1 18.4 %collective-permute-done.2 = bf16[896,512]{1,0:T(8,128)(2,1)S(1)} collective-permute-done((bf16[896,512]{1,0:T(8,128)(2,1)S(1)}, bf16[896,512]{1,0:T(8,128)(2,1)S(1)}, u32[]{:S(2)}, u32[]{:S(2)}) %collective-permute-start.2) | collective-permute-done | bytes 917536 | tf_op jit(solution)/shard_map/ppermute | solution.py:17
  103.5 23.8 %collective-permute-done.3 = bf16[896,512]{1,0:T(8,128)(2,1)S(1)} collective-permute-done((bf16[896,512]{1,0:T(8,128)(2,1)S(1)}, bf16[896,512]{1,0:T(8,128)(2,1)S(1)}, u32[]{:S(2)}, u32[]{:S(2)}) %collective-permute-start.3) | collective-permute-done | bytes 917536 | tf_op jit(solution)/shard_map/ppermute | solution.py:19
  127.3 1.8 pad_maximum_fusion.1
  129.1 9.5 %gather_fusion.1 = bf16[120,128,512]{2,1,0:T(8,128)(2,1)} fusion(bf16[22,128,512]{2,1,0:T(8,128)(2,1)} %bitcast.61, s32[1024]{0:T(1024)S(1)} %pad_clamp_fusion), kind=kCustom, calls=%fused_computation.1 | custom fusion | bytes 31457760 | tf_op jit(solution)/shard_map/gather | solution.py:33
  138.6 9.0 %bitcast_convert_fusion = bf16[8,512,128]{1,2,0:T(8,128)(2,1)S(1)} fusion(bf16[8,15,128,512]{3,2,1,0:T(8,128)(2,1)} %bitcast.63, bf16[1,8,15,128,128]{4,3,2,1,0:T(8,128)(2,1)} %param.8), kind=kOutput, calls=%fused_computation.11 | convolution fusion | flops 2013790208 | bytes 20709376 | tf_op jit(solution)/shard_map/rkab,rkbf->raf/dot_general | solution.py:34
  147.7 1.0 copy-done.1
  148.6 1.7 convolution_bitcast_fusion
  150.4 1.5 multiply_convert_fusion
  151.9 1.7 fusion.12
  153.6 124.8 %all-reduce.2.cloned.1.call-done = f32[512,512]{0,1:T(8,128)} async-done(((f32[512,512]{0,1:T(8,128)}), f32[512,512]{0,1:T(8,128)}) %all-reduce.2.cloned.1.call-update) | async-done | bytes 1048592 | tf_op jit(solution)/shard_map/psum | solution.py:57
  278.4 2.5 copy.8
  (16 shorter events, 0.3 us)
Async XLA Ops:
  7.2 1.2 copy-start
  7.2 11.2 %copy-start.4 = (s32[1,8,15]{2,1,0:T(8,128)S(1)}, s32[1,8,15]{2,1,0:T(8,128)}, u32[]{:S(2)}) copy-start(s32[1,8,15]{2,1,0:T(8,128)} %param.7) | copy-start | bytes 1444
  7.2 271.2 %all-reduce.2.cloned.1.call-start = ((), (), s32[]{:S(2)}) async-start(), calls=%async_computation | async-start | bytes 2097152 | tf_op jit(solution)/shard_map/psum | solution.py:57
  11.2 24.8 %collective-permute-start = (bf16[896,512]{1,0:T(8,128)(2,1)}, bf16[896,512]{1,0:T(8,128)(2,1)}, u32[]{:S(2)}, u32[]{:S(2)}) collective-permute-start(bf16[896,512]{1,0:T(8,128)(2,1)} %get-tuple-element.8), channel_id=1, source_target_pairs={{0,1},{1,2},{2,3},{3,4},{4,5},{5,6},{6,7},{7,8},{8,9},{9,10},{10,1... | collective-permute-start | bytes 2752520 | tf_op jit(solution)/shard_map/ppermute | solution.py:17
  17.1 42.2 %collective-permute-start.1 = (bf16[896,512]{1,0:T(8,128)(2,1)S(1)}, bf16[896,512]{1,0:T(8,128)(2,1)}, u32[]{:S(2)}, u32[]{:S(2)}) collective-permute-start(bf16[896,512]{1,0:T(8,128)(2,1)S(1)} %get-tuple-element.9), channel_id=1, source_target_pairs={{1,0},{2,1},{3,2},{4,3},{5,4},{6,5},{7,6},{8,7},{9,8},{10,9},{11,1... | collective-permute-start | bytes 2752520 | tf_op jit(solution)/shard_map/ppermute | solution.py:19
  72.1 8.2 %copy-start.3 = (bf16[1,1024,512]{2,1,0:T(8,128)(2,1)S(1)}, bf16[1,1024,512]{2,1,0:T(8,128)(2,1)}, u32[]{:S(2)}) copy-start(bf16[1,1024,512]{2,1,0:T(8,128)(2,1)} %param.9) | copy-start | bytes 3145732
  81.3 22.2 %collective-permute-start.2 = (bf16[896,512]{1,0:T(8,128)(2,1)S(1)}, bf16[896,512]{1,0:T(8,128)(2,1)S(1)}, u32[]{:S(2)}, u32[]{:S(2)}) collective-permute-start(bf16[896,512]{1,0:T(8,128)(2,1)S(1)} %get-tuple-element.6), channel_id=1, source_target_pairs={{0,1},{1,2},{2,3},{3,4},{4,5},{5,6},{6,7},{7,8},{8,9},{9,10},{10,1... | collective-permute-start | bytes 2752520 | tf_op jit(solution)/shard_map/ppermute | solution.py:17
  83.8 43.5 %collective-permute-start.3 = (bf16[896,512]{1,0:T(8,128)(2,1)S(1)}, bf16[896,512]{1,0:T(8,128)(2,1)S(1)}, u32[]{:S(2)}, u32[]{:S(2)}) collective-permute-start(bf16[896,512]{1,0:T(8,128)(2,1)S(1)} %get-tuple-element.7), channel_id=1, source_target_pairs={{1,0},{2,1},{3,2},{4,3},{5,4},{6,5},{7,6},{8,7},{9,8},{10,9},{11,1... | collective-permute-start | bytes 2752520 | tf_op jit(solution)/shard_map/ppermute | solution.py:19
  147.6 1.0 copy-start.1
  150.4 1.5 copy-start.2
  150.4 1.5 copy-start.5
Sparse Core Ops, SparseCore 0:
  150.5 127.8 all-reduce.1
where the time goes:
time: 288 us
  waiting for transfers between devices  208 us (72%)
  local copies, waits for them, and re-layouts  25 us (9%)
  matrix products  22.4 us (8%)
  between operations  14.2 us (5%)
  starting transfers between devices  11 us (4%)
  other arithmetic  7.32 us (3%)
    psum x1, waiting for transfers between devices, shards(): weight_grad = lax.psum(grads, ('dp', 'blk', 'rep'))  125 us
    ppermute x2, waiting for transfers between devices, padded(): lax.ppermute(head, axis, [((i + 1) % count, i) for i in range(ends)])  47.1 us
    ppermute x2, waiting for transfers between devices, padded(): lax.ppermute(tail, axis, [(i, (i + 1) % count) for i in range(ends)])  35.9 us
    gather x2, local copies, waits for them, and re-layouts, spread(): picked = ext_blocks[local_index]  19 us
    dot_general x2, matrix products, spread(): jnp.einsum('rkab,rkbf->raf', row_vals, picked, preferred_element_type=jnp...  17.2 us
    ppermute x2, starting transfers between devices, padded(): lax.ppermute(tail, axis, [(i, (i + 1) % count) for i in range(ends)])  8.42 us
  transfers between devices with their start and end apart: 5, of which 5 were waited for; matrix products, arithmetic and copies ran while one was open for 1% of the time, Pallas kernels for 0%

commit v1 on v0

--- a/solution.py
+++ b/solution.py
@@ -54,7 +54,8 @@
     grads = lax.dot_general(
         own, dproj, (((0,), (0,)), ((), ())), preferred_element_type=jnp.float32
     )
-    weight_grad = lax.psum(grads, ("dp", "blk", "rep"))
+    one_axis = lax.psum(grads, ("blk", "rep"))
+    weight_grad = lax.psum(one_axis, "dp")
     return (jnp.stack(activ_list), jnp.stack(grad_list), weight_grad)
 
 

time: 288 us -> 291 us (1.010)
  waiting for transfers between devices: 208 us -> 211 us
    psum x1 -> x2, waiting for transfers between devices: 125 us -> 128 us  [the longest x1 110 us: shards(): one_axis = lax.psum(grads, ('blk', 'rep'))]
  transfers between devices with their start and end apart: 5 -> 6, of which waited for: 5 -> 6; matrix products, arithmetic and copies ran while one was open for 1% -> 1% of each run, Pallas kernels for 0% -> 0%
where the time goes in v1:
time: 291 us
  waiting for transfers between devices  211 us (73%)
  local copies, waits for them, and re-layouts  25 us (9%)
  matrix products  22.4 us (8%)
  between operations  14.2 us (5%)
  starting transfers between devices  11.1 us (4%)
  other arithmetic  7.32 us (3%)
    psum x1, waiting for transfers between devices, shards(): one_axis = lax.psum(grads, ('blk', 'rep'))  110 us
    ppermute x2, waiting for transfers between devices, padded(): lax.ppermute(head, axis, [((i + 1) % count, i) for i in range(ends)])  47.1 us
    ppermute x2, waiting for transfers between devices, padded(): lax.ppermute(tail, axis, [(i, (i + 1) % count) for i in range(ends)])  35.9 us
    gather x2, local copies, waits for them, and re-layouts, spread(): picked = ext_blocks[local_index]  19 us
    psum x1, waiting for transfers between devices, shards(): weight_grad = lax.psum(one_axis, 'dp')  17.8 us
    dot_general x2, matrix products, spread(): jnp.einsum('rkab,rkbf->raf', row_vals, picked, preferred_element_type=jnp...  17.2 us
    ppermute x2, starting transfers between devices, padded(): lax.ppermute(tail, axis, [(i, (i + 1) % count) for i in range(ends)])  8.42 us
  transfers between devices with their start and end apart: 6, of which 6 were waited for; matrix products, arithmetic and copies ran while one was open for 1% of the time, Pallas kernels for 0%

profile of v1, /device:TPU:0, one launch (start us, length us, event | category | flops | bytes accessed | tf_op | source)
XLA Modules:
  0.0 290.7 jit_solution(3680276255962899780)
XLA Ops:
  7.2 1.2 copy-done
  8.4 1.7 convolution_convert_fusion.1
  10.1 1.1 fusion.16
  11.2 5.9 %collective-permute-start = (bf16[896,512]{1,0:T(8,128)(2,1)}, bf16[896,512]{1,0:T(8,128)(2,1)}, u32[]{:S(2)}, u32[]{:S(2)}) collective-permute-start(bf16[896,512]{1,0:T(8,128)(2,1)} %get-tuple-element.8), channel_id=1, source_target_pairs={{0,1},{1,2},{2,3},{3,4},{4,5},{5,6},{6,7},{7,8},{8,9},{9,10},{10,1... | collective-permute-start | bytes 2752520 | tf_op jit(solution)/shard_map/ppermute | solution.py:17
  17.1 1.3 collective-permute-start.1
  18.5 17.5 %collective-permute-done = bf16[896,512]{1,0:T(8,128)(2,1)} collective-permute-done((bf16[896,512]{1,0:T(8,128)(2,1)}, bf16[896,512]{1,0:T(8,128)(2,1)}, u32[]{:S(2)}, u32[]{:S(2)}) %collective-permute-start) | collective-permute-done | bytes 917536 | tf_op jit(solution)/shard_map/ppermute | solution.py:17
  36.1 23.3 %collective-permute-done.1 = bf16[896,512]{1,0:T(8,128)(2,1)} collective-permute-done((bf16[896,512]{1,0:T(8,128)(2,1)S(1)}, bf16[896,512]{1,0:T(8,128)(2,1)}, u32[]{:S(2)}, u32[]{:S(2)}) %collective-permute-start.1) | collective-permute-done | bytes 917536 | tf_op jit(solution)/shard_map/ppermute | solution.py:19
  59.3 3.2 %pad_maximum_fusion = bf16[2816,512]{1,0:T(8,128)(2,1)} fusion(bf16[896,512]{1,0:T(8,128)(2,1)} %collective-permute-done.1, bf16[1024,512]{1,0:T(8,128)(2,1)S(1)} %convolution_convert_fusion.1, bf16[896,512]{1,0:T(8,128)(2,1)} %collective-permute-done), kind=kLoop, calls=%fused_computation.6 | loop fusion | flops 8650752 | bytes 5767168 | tf_op jit(solution)/shard_map/concatenate | solution.py:15
  62.6 9.5 %gather_fusion = bf16[120,128,512]{2,1,0:T(8,128)(2,1)} fusion(bf16[22,128,512]{2,1,0:T(8,128)(2,1)} %bitcast.62, s32[1024]{0:T(1024)S(1)} %pad_clamp_fusion), kind=kCustom, calls=%fused_computation | custom fusion | bytes 31457760 | tf_op jit(solution)/shard_map/gather | solution.py:33
  72.1 8.2 %fusion = f32[8,512,128,1]{1,2,3,0:T(8,128)S(1)} fusion(bf16[8,15,128,512]{3,2,1,0:T(8,128)(2,1)} %bitcast.64, bf16[1,8,15,128,128]{4,3,2,1,0:T(8,128)(2,1)} %param.8), kind=kOutput, calls=%fused_computation.2 | convolution fusion | flops 2013265920 | bytes 21757952 | tf_op jit(solution)/shard_map/rkab,rkbf->raf/dot_general | solution.py:34
  81.3 2.5 collective-permute-start.2
  83.8 1.3 collective-permute-start.3
  85.1 18.4 %collective-permute-done.2 = bf16[896,512]{1,0:T(8,128)(2,1)S(1)} collective-permute-done((bf16[896,512]{1,0:T(8,128)(2,1)S(1)}, bf16[896,512]{1,0:T(8,128)(2,1)S(1)}, u32[]{:S(2)}, u32[]{:S(2)}) %collective-permute-start.2) | collective-permute-done | bytes 917536 | tf_op jit(solution)/shard_map/ppermute | solution.py:17
  103.5 23.8 %collective-permute-done.3 = bf16[896,512]{1,0:T(8,128)(2,1)S(1)} collective-permute-done((bf16[896,512]{1,0:T(8,128)(2,1)S(1)}, bf16[896,512]{1,0:T(8,128)(2,1)S(1)}, u32[]{:S(2)}, u32[]{:S(2)}) %collective-permute-start.3) | collective-permute-done | bytes 917536 | tf_op jit(solution)/shard_map/ppermute | solution.py:19
  127.3 1.8 pad_maximum_fusion.1
  129.1 9.5 %gather_fusion.1 = bf16[120,128,512]{2,1,0:T(8,128)(2,1)} fusion(bf16[22,128,512]{2,1,0:T(8,128)(2,1)} %bitcast.61, s32[1024]{0:T(1024)S(1)} %pad_clamp_fusion), kind=kCustom, calls=%fused_computation.1 | custom fusion | bytes 31457760 | tf_op jit(solution)/shard_map/gather | solution.py:33
  138.6 9.0 %bitcast_convert_fusion = bf16[8,512,128]{1,2,0:T(8,128)(2,1)S(1)} fusion(bf16[8,15,128,512]{3,2,1,0:T(8,128)(2,1)} %bitcast.63, bf16[1,8,15,128,128]{4,3,2,1,0:T(8,128)(2,1)} %param.8), kind=kOutput, calls=%fused_computation.11 | convolution fusion | flops 2013790208 | bytes 20709376 | tf_op jit(solution)/shard_map/rkab,rkbf->raf/dot_general | solution.py:34
  147.7 1.0 copy-done.1
  148.6 1.7 convolution_bitcast_fusion
  150.4 109.9 %all-reduce.3.cloned.1.call-done = f32[512,512]{0,1:T(8,128)} async-done(((f32[512,512]{0,1:T(8,128)}), f32[512,512]{0,1:T(8,128)}) %all-reduce.3.cloned.1.call-update) | async-done | bytes 1048592 | tf_op jit(solution)/shard_map/psum | solution.py:57
  260.4 1.5 multiply_convert_fusion
  261.9 1.7 fusion.12
  263.6 17.8 %all-reduce.5.cloned.1.call-done = f32[512,512]{0,1:T(8,128)} async-done(((f32[512,512]{0,1:T(8,128)}), f32[512,512]{0,1:T(8,128)}) %all-reduce.5.cloned.1.call-update) | async-done | bytes 1048592 | tf_op jit(solution)/shard_map/psum | solution.py:58
  281.4 2.5 copy.8
  (19 shorter events, 1.2 us)
Async XLA Ops:
  7.2 1.2 copy-start
  7.2 11.2 %copy-start.4 = (s32[1,8,15]{2,1,0:T(8,128)S(1)}, s32[1,8,15]{2,1,0:T(8,128)}, u32[]{:S(2)}) copy-start(s32[1,8,15]{2,1,0:T(8,128)} %param.7) | copy-start | bytes 1444
  7.2 253.1 %all-reduce.3.cloned.1.call-start = ((), (), s32[]{:S(2)}) async-start(), calls=%async_computation | async-start | bytes 2097152 | tf_op jit(solution)/shard_map/psum | solution.py:57
  11.2 24.8 %collective-permute-start = (bf16[896,512]{1,0:T(8,128)(2,1)}, bf16[896,512]{1,0:T(8,128)(2,1)}, u32[]{:S(2)}, u32[]{:S(2)}) collective-permute-start(bf16[896,512]{1,0:T(8,128)(2,1)} %get-tuple-element.8), channel_id=1, source_target_pairs={{0,1},{1,2},{2,3},{3,4},{4,5},{5,6},{6,7},{7,8},{8,9},{9,10},{10,1... | collective-permute-start | bytes 2752520 | tf_op jit(solution)/shard_map/ppermute | solution.py:17
  17.1 42.2 %collective-permute-start.1 = (bf16[896,512]{1,0:T(8,128)(2,1)S(1)}, bf16[896,512]{1,0:T(8,128)(2,1)}, u32[]{:S(2)}, u32[]{:S(2)}) collective-permute-start(bf16[896,512]{1,0:T(8,128)(2,1)S(1)} %get-tuple-element.9), channel_id=1, source_target_pairs={{1,0},{2,1},{3,2},{4,3},{5,4},{6,5},{7,6},{8,7},{9,8},{10,9},{11,1... | collective-permute-start | bytes 2752520 | tf_op jit(solution)/shard_map/ppermute | solution.py:19
  72.1 8.2 %copy-start.3 = (bf16[1,1024,512]{2,1,0:T(8,128)(2,1)S(1)}, bf16[1,1024,512]{2,1,0:T(8,128)(2,1)}, u32[]{:S(2)}) copy-start(bf16[1,1024,512]{2,1,0:T(8,128)(2,1)} %param.9) | copy-start | bytes 3145732
  81.3 22.2 %collective-permute-start.2 = (bf16[896,512]{1,0:T(8,128)(2,1)S(1)}, bf16[896,512]{1,0:T(8,128)(2,1)S(1)}, u32[]{:S(2)}, u32[]{:S(2)}) collective-permute-start(bf16[896,512]{1,0:T(8,128)(2,1)S(1)} %get-tuple-element.6), channel_id=1, source_target_pairs={{0,1},{1,2},{2,3},{3,4},{4,5},{5,6},{6,7},{7,8},{8,9},{9,10},{10,1... | collective-permute-start | bytes 2752520 | tf_op jit(solution)/shard_map/ppermute | solution.py:17
  83.8 43.5 %collective-permute-start.3 = (bf16[896,512]{1,0:T(8,128)(2,1)S(1)}, bf16[896,512]{1,0:T(8,128)(2,1)S(1)}, u32[]{:S(2)}, u32[]{:S(2)}) collective-permute-start(bf16[896,512]{1,0:T(8,128)(2,1)S(1)} %get-tuple-element.7), channel_id=1, source_target_pairs={{1,0},{2,1},{3,2},{4,3},{5,4},{6,5},{7,6},{8,7},{9,8},{10,9},{11,1... | collective-permute-start | bytes 2752520 | tf_op jit(solution)/shard_map/ppermute | solution.py:19
  147.6 1.0 copy-start.1
  150.3 131.0 %all-reduce.5.cloned.1.call-start = ((), (), s32[]{:S(2)}) async-start(), calls=%async_computation.1 | async-start | bytes 2097152 | tf_op jit(solution)/shard_map/psum | solution.py:58
  260.3 1.5 copy-start.2
  260.4 1.5 copy-start.5
Sparse Core Ops, SparseCore 0:
  150.5 109.8 all-reduce.2
  262.7 18.6 all-reduce.4
